TPU v7x, 128 devices: a whole 4x4x4 slice. The times are simulated.
128 devices in a mesh: img: 4 (over y_hi, core), gz: 32 (over x, y_lo, z).
Axes of the slice: x: 4, y: 4 (y_hi: 2, y_lo: 2; y = y_hi * 2 + y_lo), z: 4, core: 2. Of those that a mesh axis runs over, the one named last changes fastest.
Arguments:
- images: float32 [16, 5, 64, 128, 128], P('img', None, 'gz'), may hold values from -12 to 12
- centre: int32 [16], P('img'), may hold values from 1 to 14, as said below
- positions: float32 [16], P('img'), may hold values from 0 to 1
Outputs:
- path: float32 [16, 5, 64, 128, 128], P('img', None, 'gz')
Inputs may be any that keep to these rules, and one draw needn't show every extreme that they name: `centre`: centre_m lies within m - 1 to m + 1, clipped to 1 to 14; at the first target of each aligned block of 4 it is m - 1 and at the last m + 1, before clipping.
All inputs are finite; a program needn't handle non-finite values.
Results may differ from a plain program's by a relative error of at most 0.0003.
Values sent between devices are 32-bit elements; how exact they have to be, the bound alone decides.
No kernel may reach another device: no remote copies, remote signals or barrier semaphores. Data moves between devices by JAX's collectives and lax.ppermute only.
A program may use at most 64 MiB of HBM per device.

v0:
```python
import functools

import jax
import jax.numpy as jnp
import numpy as np
from jax import lax
from jax.experimental import pallas as pl
from jax.experimental.pallas import tpu as pltpu
from jax.sharding import PartitionSpec as P

NX = 128
NY = 128
NZ = 64
GROUPS = 32
IMAGES = 16
LOCAL = 4
CELLS = 5.0 * NZ * NX * NY
SMOOTH = 64.0
EPS = 1e-6
KEEP = 1.0 - 1.0 / SMOOTH
SLOTS = 5
FORWARD_MIB = 56
SOLVE_MIB = 16
INVERSE_MIB = 8
EDGE_MIB = 4
FINAL_MIB = 16
F32 = jnp.float32
BF16 = jnp.bfloat16


def real_basis(length):
    k = np.arange(length)[:, None]
    x = np.arange(length)[None, :]
    angle = 2.0 * np.pi * ((k * x) % length) / length
    table = np.where(k <= length // 2, np.cos(angle), np.sin(angle)) * np.sqrt(2.0 / length)
    table[0] = 1.0 / np.sqrt(length)
    table[length // 2] = np.cos(np.pi * np.arange(length)) / np.sqrt(length)
    return table


def split_np(table):
    import ml_dtypes

    high = table.astype(ml_dtypes.bfloat16)
    low = (table - high.astype(np.float64)).astype(ml_dtypes.bfloat16)
    return high, low


def right_table(table):
    high, low = split_np(table)
    row = np.concatenate([high, low], axis=1)
    return np.concatenate([row, row], axis=0)


def left_table(table):
    high, low = split_np(table)
    return np.concatenate([high, high, low], axis=1)


@functools.cache
def tables():
    basis_x = real_basis(NX)
    basis_y = real_basis(NY)
    swap = np.arange(NX).reshape(-1, 2, 4)[:, ::-1].reshape(-1)
    forward_y = right_table(0.25 * basis_y.T)
    inverse_y = right_table(basis_y)
    forward_x = np.stack([left_table(basis_x), left_table(basis_x[swap])])
    inverse_x = np.stack([left_table(basis_x.T), left_table(basis_x[swap].T)])
    device = np.arange(GROUPS)[:, None]
    row = np.arange(8)[None, :] % 4
    wave_x = 8 * (device % 16) + 4 * (device // 16) + row
    lam_x = 2.0 - 2.0 * np.cos(2.0 * np.pi * wave_x / NX)
    lam_y = 2.0 - 2.0 * np.cos(2.0 * np.pi * np.arange(NY) / NY)
    lam = lam_x[:, :, None] + lam_y[None, None, :]
    excess = 0.5 / SMOOTH + 0.5 * lam
    rho = 1.0 / (1.0 + excess + np.sqrt(excess * (excess + 2.0)))
    return forward_y, inverse_y, forward_x, inverse_x, rho.astype(np.float32)


def split(value):
    high = value.astype(BF16)
    low = (value - high.astype(F32)).astype(BF16)
    return high, low


def times_right(value, table):
    high, low = split(value)
    both = jnp.dot(jnp.concatenate([high, low], axis=1), table, preferred_element_type=F32)
    return both[:, :128] + both[:, 128:]


def shifts(f, axis):
    size = NX if axis == 0 else NY
    return pltpu.roll(f, size - 1, axis), pltpu.roll(f, 1, axis)


def local_drive(q):
    q1, q2, q3, q4, q5 = q
    d1, d2, d3, d4, d5 = (f + f for f in q)
    square = d2 * q2
    s11 = d1 * q1 + (square + d3 * q3)
    s22 = d4 * q4 + (square + d5 * q5)
    trace = (s11 + s22) + (d1 * q4 - square)
    scale = 4.0 * (0.2 + 1.0 / SMOOTH) - 0.4 * trace
    third = trace * (2.0 / 3.0)
    rolled = {}
    for name, f in (("2", q2), ("3", q3), ("5", q5)):
        for axis in range(2):
            rolled[name, axis] = shifts(f, axis)

    def step(name, axis):
        after, before = rolled[name, axis]
        return after - before

    after, before = shifts(d1 + q4, 1)
    step_y = after - before
    after, before = shifts(q1 + d4, 0)
    step_x = after - before
    f1 = scale * q1 + ((s11 - third) - 2.0 * step("3", 1))
    f2 = q2 * (scale + (d1 + d4)) + (d3 * q5 + (step("3", 0) - step("5", 1)))
    f3 = q3 * (scale - d4) + (d2 * q5 + (step_y - step("2", 0)))
    f4 = scale * q4 + ((s22 - third) + 2.0 * step("5", 0))
    f5 = q5 * (scale - d1) + (d2 * q3 + (step("2", 1) - step_x))
    return (f1, f2, f3, f4, f5), rolled


def mixed(q):
    return q[1], q[0] - q[3], q[4], q[2]


def add_spread(f, r, factor):
    whole_part = [value if factor in (1, -1) else abs(factor) * value for value in r]
    twice = (2.0 * abs(factor)) * r[0]
    if factor < 0:
        return (
            f[0] - twice,
            f[1] + whole_part[1],
            f[2] - whole_part[2],
            f[3] + twice,
            f[4] + whole_part[3],
        )
    return (
        f[0] + twice,
        f[1] - whole_part[1],
        f[2] + whole_part[2],
        f[3] - twice,
        f[4] - whole_part[3],
    )


def along_plane(f, x, y):
    return (6.0 + 1.0 / SMOOTH) * f - ((x[0] + x[1]) + (y[0] + y[1]))


def push(stack, slot, half, value):
    h, l = split(value)
    cols = slice(half * 128, half * 128 + 128)
    stack[slot, 0:128, cols] = h
    stack[slot, 128:256, cols] = l
    stack[slot, 256:384, cols] = h


def forward_kernel(
    where,
    img_hbm,
    ty_hbm,
    tx_hbm,
    rho_hbm,
    out,
    keep,
    mine,
    img,
    img_sem,
    ty,
    tx,
    rho_ref,
    table_sem,
    stack,
    spectrum,
):
    def fetch(n):
        return pltpu.make_async_copy(img_hbm.at[n], img.at[n], img_sem.at[n])

    small = [
        pltpu.make_async_copy(source, target, table_sem.at[n])
        for n, (source, target) in enumerate(((ty_hbm, ty), (tx_hbm, tx), (rho_hbm, rho_ref)))
    ]
    fetch(0).start()
    for copy in small:
        copy.start()
    for n in range(1, LOCAL):
        fetch(n).start()
    for copy in small:
        copy.wait()
    mine[...] = rho_ref[where[0]]

    @pl.loop(0, 2)
    def _(pair):
        for i in range(2):
            fetch(2 * pair + i).wait()
        for i in range(2):
            qe = [img[2 * pair + i, c, 0] for c in range(5)]
            qo = [img[2 * pair + i, c, 1] for c in range(5)]
            re = mixed(qe)
            ro = mixed(qo)
            f, _ = local_drive(qe)
            for c, value in enumerate(add_spread(f, ro, 2)):
                push(stack, c, 0, times_right(value, ty[...]))
            f, rolled = local_drive(qo)
            total = [re[1] + along_plane(ro[1], shifts(ro[1], 0), shifts(ro[1], 1))]
            for r, name in ((0, "2"), (2, "5"), (3, "3")):
                total.append(re[r] + along_plane(ro[r], rolled[name, 0], rolled[name, 1]))
            total = (total[1], total[0], total[2], total[3])
            for c, value in enumerate(add_spread(f, total, -1)):
                push(stack, c, 1, times_right(value, ty[...]))
            for r in range(4):
                push(stack, 5 + r // 2, r % 2, times_right(re[r], ty[...]))
            for n in range(7):
                spectrum[i, n] = jnp.dot(tx[i], stack[n], preferred_element_type=F32)
        first = lax.broadcasted_iota(jnp.int32, (16, 8, 128), 1) < 4
        for part in range(2):
            rows = slice(part * 16, part * 16 + 16)
            rho = rho_ref[rows]
            beta = rho + 1.0 / rho
            back = (1.0 / SMOOTH) / beta

            def tile(n, half):
                cols = slice(half * 128, half * 128 + 128)
                a = spectrum[0, n, :, cols].reshape(16, 8, 128)
                b = spectrum[1, n, :, cols].reshape(16, 8, 128)
                return jnp.where(first, a, b) if part == 0 else jnp.where(first, b, a)

            g = [beta * tile(5 + r // 2, r % 2) for r in range(4)]
            ys = [tile(c, 0) for c in range(5)]
            ks = add_spread(ys, g, 1)
            for c in range(5):
                y = ys[c]
                out[rows, 0, pair, c] = beta * tile(c, 1) + y
                out[rows, 1, pair, c] = ks[c]
                keep[pair, c, rows] = back * y


def solve_kernel(f, rho_ref, out, right, work):
    rho = rho_ref[...]
    sigma = rho * rho
    power = sigma
    for _ in range(5):
        power = power * power
    closing = 1.0 / (1.0 - power)
    shape = (2, 5, 8, 128)
    zero = jnp.zeros(shape, F32)
    sb = jnp.broadcast_to(sigma, shape)
    cb = jnp.broadcast_to(closing, shape)

    def ends(s, carry):
        v, u, p = carry
        r = f[s, 0] + f[lax.rem(s + 1, GROUPS), 1]
        right[s] = r
        return r + sb * v, u + p[None, None] * r, p * sigma

    v, u, _ = lax.fori_loop(0, GROUPS, ends, (zero, zero, jnp.ones((8, 128), F32)))
    u_last = u * cb

    def up(s, v):
        v = right[s] + sb * v
        work[s] = v
        return v

    lax.fori_loop(0, GROUPS, up, v * cb)
    gain = jnp.broadcast_to(sigma / (1.0 - sigma * sigma), shape)
    back = jnp.broadcast_to((1.0 / SMOOTH) / (rho + 1.0 / rho), shape)

    def put(s, slot, value):
        out[s, :, :, slot] = value

    def down(n, carry):
        u, after = carry
        s = GROUPS - 1 - n
        value = sb * u
        p = gain * (work[s] + value)
        put(s, 0, p)
        put(s + 1, 1, back * (p + after))
        return right[s] + value, p

    value = sb * u_last
    last = gain * (work[GROUPS - 1] + value)
    put(GROUPS - 1, 0, last)
    _, head = lax.fori_loop(1, GROUPS, down, (right[GROUPS - 1] + value, last))
    put(0, 1, back * (head + last))


def fold(value):
    return jnp.sum((value * value).reshape(16, 8, 128), axis=0)


def inverse_kernel(*refs, chosen):
    spec, keep, img, ty, tx = refs[:5]
    stack = refs[-1]
    if chosen[0] == 0:
        out = [refs[5]]
        start = None
    else:
        start, second, upper, sums = refs[5:9]
        out = [second, upper.at[0], upper.at[1]]
        sums[...] = jnp.zeros_like(sums)
    first = lax.broadcasted_iota(jnp.int32, (16, 8, 128), 1) < 4

    mixes = ((1, 0.5), (0, -0.25), (4, 0.25), (1, -0.5), (2, -0.25))
    for c in range(5):
        source, weight = mixes[c]
        weight = weight / SMOOTH
        if start is not None:
            last = (start[c, 0], start[c, 1])
        for n, image in enumerate(chosen):
            pair, i = image // 2, image % 2
            p_even, p_odd = spec[0:16, pair, c, 0], spec[16:32, pair, c, 0]
            w_even = spec[0:16, pair, c, 1] + keep[pair, c, 0:16]
            w_odd = spec[16:32, pair, c, 1] + keep[pair, c, 16:32]
            if i == 1:
                p_even, p_odd, w_even, w_odd = p_odd, p_even, w_odd, w_even
            slot = (c * len(chosen) + n) % SLOTS
            push(stack, slot, 0, jnp.where(first, w_even, w_odd).reshape(128, 128))
            push(stack, slot, 1, jnp.where(first, p_even, p_odd).reshape(128, 128))
            both = jnp.dot(tx[i], stack[slot], preferred_element_type=F32)
            even = KEEP * img[image, c, 0] + times_right(both[:, :128], ty[...])
            odd = times_right(both[:, 128:], ty[...])
            mix = img[image, source, 1]
            if c == 1:
                mix = mix - img[image, 3, 1]
            odd = KEEP * img[image, c, 1] + odd * (1.0 / SMOOTH) + weight * mix
            out[n][c, 0] = even
            out[n][c, 1] = odd
            if start is not None:
                sums[n] += fold(even - last[0]) + fold(odd - last[1])
                last = (even, odd)


def edge_kernel(sums, upper, above, out):
    edge = jnp.zeros((8, 128), F32)
    for c in range(5):
        for zz in range(2):
            edge = edge + fold(above[c, zz] - upper[1, c, zz])
    rows = [sums[0], sums[1], sums[2], edge]
    index = lax.broadcasted_iota(jnp.int32, (1, 128), 1)
    total = jnp.zeros((1, 128), F32)
    for g, row in enumerate(rows):
        total = jnp.where(index == g, jnp.sum(row), total)
    out[...] = jnp.broadcast_to(total, (128, 1, 128))


def final_kernel(
    centre,
    positions,
    where,
    sums,
    below_hbm,
    s0,
    s1,
    upper,
    a0,
    a1_hbm,
    out_hbm,
    below,
    a1,
    out,
    below_sem,
    a1_sem,
    out_sem,
):
    def fetch_below(c):
        return pltpu.make_async_copy(below_hbm.at[:, c], below.at[c], below_sem.at[c])

    def fetch_a1(c):
        return pltpu.make_async_copy(a1_hbm.at[c], a1.at[c], a1_sem.at[c])

    def store(c):
        return pltpu.make_async_copy(out.at[c], out_hbm.at[:, c], out_sem.at[c])

    for c in range(5):
        fetch_below(c).start()
        fetch_a1(c).start()
    arc = [jnp.zeros((8, 128), F32)]
    lane = lax.broadcasted_iota(jnp.int32, (1, 128), 1)
    for k in range(LOCAL):
        block = jnp.sum(sums[k * GROUPS : (k + 1) * GROUPS], axis=0)
        dist = jnp.sqrt(block * (1.0 / CELLS) + EPS)
        for g in range(4):
            if k * 4 + g < IMAGES - 1:
                value = jnp.sum(jnp.where(lane == g, dist, 0.0), axis=1, keepdims=True)
                arc.append(arc[-1] + jnp.broadcast_to(value, (8, 128)))
    base = where[0] * LOCAL - 2
    weights = {}
    for m in range(LOCAL):
        c = centre[m]
        tau = positions[m] * arc[-1]

        def pick(index):
            value = arc[0]
            for j in range(1, IMAGES):
                value = jnp.where(index == j, arc[j], value)
            return value

        a, b, d = pick(c - 1), pick(c), pick(c + 1)
        w = (
            (tau - b) * (tau - d) / ((a - b) * (a - d)),
            (tau - a) * (tau - d) / ((b - a) * (b - d)),
            (tau - a) * (tau - b) / ((d - a) * (d - b)),
        )
        for r in range(5):
            spot = base + m + r
            value = jnp.zeros((8, 128), F32)
            for n in range(3):
                value = jnp.where(c - 1 + n == spot, w[n], value)
            weights[m, r] = value

    for c in range(5):
        fetch_below(c).wait()
        fetch_a1(c).wait()
        lines = [below.at[c, 0], below.at[c, 1], s0.at[c], s1.at[c]]
        lines += [upper.at[0, c], upper.at[1, c], a0.at[c], a1.at[c]]
        for zz in range(2):
            for n in range(16):
                rows = slice(8 * n, 8 * n + 8)
                pieces = [line[zz, rows] for line in lines]
                for m in range(LOCAL):
                    acc = pieces[m] * weights[m, 0]
                    for r in range(1, 5):
                        acc = acc + pieces[m + r] * weights[m, r]
                    out[c, m, zz, rows] = acc
        store(c).start()
    for c in range(5):
        store(c).wait()


SMEM = pl.BlockSpec(memory_space=pltpu.SMEM)
VMEM = pl.BlockSpec(memory_space=pltpu.VMEM)
HBM = pl.BlockSpec(memory_space=pltpu.HBM)


def plain(mib):
    return pltpu.CompilerParams(vmem_limit_bytes=mib * 1024 * 1024)


def cost(flops, moved):
    return pl.CostEstimate(flops=flops, bytes_accessed=moved, transcendentals=0)


def forward(images, ty, tx, rho):
    where = lax.axis_index("gz").astype(jnp.int32).reshape(1)
    return pl.pallas_call(
        forward_kernel,
        out_shape=(
            pltpu.VMEM((GROUPS, 2, 2, 5, 8, 128), F32),
            pltpu.VMEM((2, 5, GROUPS, 8, 128), F32),
            pltpu.VMEM((8, 128), F32),
        ),
        in_specs=[SMEM, HBM, HBM, HBM, HBM],
        out_specs=(VMEM,) * 3,
        scratch_shapes=[
            pltpu.VMEM((LOCAL, 5, 2, 128, 128), F32),
            pltpu.SemaphoreType.DMA((LOCAL,)),
            pltpu.VMEM((256, 256), BF16),
            pltpu.VMEM((2, 128, 384), BF16),
            pltpu.VMEM((GROUPS, 8, 128), F32),
            pltpu.SemaphoreType.DMA((3,)),
            pltpu.VMEM((7, 384, 256), BF16),
            pltpu.VMEM((2, 7, 128, 256), F32),
        ],
        compiler_params=plain(FORWARD_MIB),
        cost_estimate=cost(3_000_000_000, 9_000_000),
        name="forward",
    )(where, images, ty, tx, rho)


def solve(f, rho):
    return pl.pallas_call(
        solve_kernel,
        out_shape=pltpu.VMEM((GROUPS, 2, 5, 2, 8, 128), F32),
        in_specs=[VMEM, VMEM],
        out_specs=VMEM,
        scratch_shapes=[
            pltpu.VMEM((GROUPS, 2, 5, 8, 128), F32),
            pltpu.VMEM((GROUPS, 2, 5, 8, 128), F32),
        ],
        compiler_params=plain(SOLVE_MIB),
        cost_estimate=cost(20_000_000, 6_000_000),
        name="solve",
    )(f, rho)


def inverse(chosen, spec, keep, images, ty, tx, *start):
    one = pltpu.VMEM((5, 2, 128, 128), F32)
    if start:
        out_shape = (one, pltpu.VMEM((2, 5, 2, 128, 128), F32), pltpu.VMEM((3, 8, 128), F32))
    else:
        out_shape = (one,)
    args = (spec, keep, images, ty, tx, *start)
    count = len(chosen)
    return pl.pallas_call(
        functools.partial(inverse_kernel, chosen=chosen),
        out_shape=out_shape,
        in_specs=[VMEM] * len(args),
        out_specs=(VMEM,) * len(out_shape),
        scratch_shapes=[pltpu.VMEM((SLOTS, 384, 256), BF16)],
        compiler_params=plain(INVERSE_MIB),
        cost_estimate=cost(1_000_000_000 * count, 3_000_000 * count),
        name="inverse",
    )(*args)


def edge(sums, upper, above):
    return pl.pallas_call(
        edge_kernel,
        out_shape=pltpu.VMEM((128, 1, 128), F32),
        in_specs=[VMEM] * 3,
        out_specs=VMEM,
        compiler_params=plain(EDGE_MIB),
        cost_estimate=cost(2_000_000, 1_300_000),
        name="edge",
    )(sums, upper, above)


def final(centre, positions, sums, below, s0, s1, upper, a0, a1):
    where = lax.axis_index("img").astype(jnp.int32).reshape(1)
    return pl.pallas_call(
        final_kernel,
        out_shape=jax.ShapeDtypeStruct((4, 5, 2, 128, 128), F32),
        in_specs=[SMEM, SMEM, SMEM, VMEM, HBM, VMEM, VMEM, VMEM, VMEM, HBM],
        out_specs=HBM,
        scratch_shapes=[
            pltpu.VMEM((5, 2, 2, 128, 128), F32),
            pltpu.VMEM((5, 2, 128, 128), F32),
            pltpu.VMEM((5, 4, 2, 128, 128), F32),
            pltpu.SemaphoreType.DMA((5,)),
            pltpu.SemaphoreType.DMA((5,)),
            pltpu.SemaphoreType.DMA((5,)),
        ],
        compiler_params=plain(FINAL_MIB),
        cost_estimate=cost(30_000_000, 8_000_000),
        name="final",
    )(centre, positions, where, sums, below, s0, s1, upper, a0, a1)


def local(images, centre, positions):
    forward_y, inverse_y, forward_x, inverse_x, rho = (jnp.asarray(t) for t in tables())
    rows = [(i, i + 1) for i in range(LOCAL - 1)]
    rows_back = [(b, a) for a, b in rows]
    f, keep, mine = forward(images, forward_y, forward_x, rho)
    f = lax.all_to_all(f, "gz", 0, 0, tiled=True)
    u = solve(f, mine)
    u = lax.all_to_all(u, "gz", 0, 0, tiled=True)
    (s0,) = inverse((0,), u, keep, images, inverse_y, inverse_x)
    a0 = lax.ppermute(s0, "img", rows_back)
    s1, upper, sums = inverse((1, 2, 3), u, keep, images, inverse_y, inverse_x, s0)
    a1 = lax.ppermute(s1, "img", rows_back)
    below = lax.ppermute(upper, "img", rows)
    part = edge(sums, upper, a0)
    sums = lax.all_to_all(part, ("img", "gz"), 0, 0, tiled=True)
    return final(centre, positions, sums, below, s0, s1, upper, a0, a1)


def solution(mesh):
    in_specs = (P("img", None, "gz", None, None), P("img"), P("img"))
    out_specs = P("img", None, "gz", None, None)
    return jax.shard_map(
        local, mesh=mesh, in_specs=in_specs, out_specs=out_specs, check_vma=False
    )
```

profile of v0, /device:TPU:1, one launch (start us, length us, event | category | flops | bytes accessed | tf_op | source)
XLA Modules:
  0.0 126.5 jit_solution(12175741497213334364)
XLA Ops:
  0.0 5.5 %forward.1 = (f32[32,2,2,5,8,128]{5,4,3,2,1,0:T(8,128)S(1)}, f32[2,5,32,8,128]{4,3,2,1,0:T(8,128)S(1)}, f32[8,128]{1,0:T(8,128)S(1)}) custom-call(s32[1]{0:T(128)} %bitcast.1.where, f32[4,5,2,128,128]{4,3,2,1,0:T(8,128)} %refs_2_.3, bf16[256,256]{1,0:T(8,128)(2,1)} %constant.19.clone.ty_hbm, bf16[2,128,384]{2,1,0:T(8,128)(2,1)} %constant.21.clone.tx_hbm, ...), custom_call_target="tpu_custom_call" | custom-call | flops 3000000000 | bytes 9000000 | tf_op jit(solution)/shard_map/forward/pallas_call | solution.py:450
  5.5 41.9 %all_to_all.15.f = f32[32,2,2,5,8,128]{5,4,3,2,1,0:T(8,128)S(1)} all-to-all(f32[32,2,2,5,8,128]{5,4,3,2,1,0:T(8,128)S(1)} %get-tuple-element.11), channel_id=1, replica_groups=mesh['img'=4,'gz'=32] {'gz'}, dimensions={0} | all-to-all | bytes 5242880 | tf_op jit(solution)/shard_map/all_to_all | solution.py:549
  47.4 1.1 solve.1
  48.5 0.0 copy-start
  48.5 0.0 copy-start.1
  48.6 0.0 copy-start.2
  48.6 36.8 %all_to_all.16.refs_0_ = f32[32,2,5,2,8,128]{5,4,3,2,1,0:T(8,128)S(1)} all-to-all(f32[32,2,5,2,8,128]{5,4,3,2,1,0:T(8,128)S(1)} %solve.1), channel_id=1, replica_groups=mesh['img'=4,'gz'=32] {'gz'}, dimensions={0} | all-to-all | bytes 5242880 | tf_op jit(solution)/shard_map/all_to_all | solution.py:551
  85.4 0.0 copy-done
  85.4 0.0 copy-done.1
  85.4 0.7 inverse.2.refs_5_.s0
  86.1 0.0 copy-start.3
  86.1 0.0 copy-start.4
  86.1 2.0 %inverse.3 = (f32[5,2,128,128]{3,2,1,0:T(8,128)S(1)}, f32[2,5,2,128,128]{4,3,2,1,0:T(8,128)S(1)}, f32[3,8,128]{2,1,0:T(8,128)S(1)}) custom-call(f32[32,2,5,2,8,128]{5,4,3,2,1,0:T(8,128)S(1)} %all_to_all.16.refs_0_, f32[2,5,32,8,128]{4,3,2,1,0:T(8,128)S(1)} %get-tuple-element.13.refs_1_, f32[4,5,2,128,128]{4,3,2,1,0:T(8,128)S(1)} %copy-done, ...), custom_call_target="tpu_custom_call" | custom-call | flops 3000000000 | bytes 9000000 | tf_op jit(solution)/shard_map/inverse/pallas_call | solution.py:499
  88.2 7.8 %collective-permute-start.1 = (f32[2,5,2,128,128]{4,3,2,1,0:T(8,128)S(1)}, f32[2,5,2,128,128]{4,3,2,1,0:T(8,128)}, u32[]{:S(2)}, u32[]{:S(2)}) collective-permute-start(f32[2,5,2,128,128]{4,3,2,1,0:T(8,128)S(1)} %get-tuple-element.15.upper), channel_id=1, source_target_pairs={{0,32},{32,64},{64,96},{1,33},{33,65},{65,97},{2,34},{34,66},{66,9... | collective-permute-start | bytes 3932168 | tf_op jit(solution)/shard_map/ppermute | solution.py:556
  95.9 1.9 %collective-permute-start = (f32[5,2,128,128]{3,2,1,0:T(8,128)S(1)}, f32[5,2,128,128]{3,2,1,0:T(8,128)S(1)}, u32[]{:S(2)}, u32[]{:S(2)}) collective-permute-start(f32[5,2,128,128]{3,2,1,0:T(8,128)S(1)} %inverse.2.refs_5_.s0), channel_id=1, source_target_pairs={{32,0},{64,32},{96,64},{33,1},{65,33},{97,65},{34,2},{66,34},{98,6... | collective-permute-start | bytes 1966088 | tf_op jit(solution)/shard_map/ppermute | solution.py:553
  97.9 1.9 %collective-permute-start.2 = (f32[5,2,128,128]{3,2,1,0:T(8,128)S(1)}, f32[5,2,128,128]{3,2,1,0:T(8,128)}, u32[]{:S(2)}, u32[]{:S(2)}) collective-permute-start(f32[5,2,128,128]{3,2,1,0:T(8,128)S(1)} %get-tuple-element.16.s1), channel_id=1, source_target_pairs={{32,0},{64,32},{96,64},{33,1},{65,33},{97,65},{34,2},{66,34},{98,6... | collective-permute-start | bytes 1966088 | tf_op jit(solution)/shard_map/ppermute | solution.py:555
  99.8 9.6 %collective-permute-done.above.a0 = f32[5,2,128,128]{3,2,1,0:T(8,128)S(1)} collective-permute-done((f32[5,2,128,128]{3,2,1,0:T(8,128)S(1)}, f32[5,2,128,128]{3,2,1,0:T(8,128)S(1)}, u32[]{:S(2)}, u32[]{:S(2)}) %collective-permute-start) | collective-permute-done | bytes 655392 | tf_op jit(solution)/shard_map/ppermute | solution.py:553
  109.3 0.8 edge.1
  110.2 3.5 %all-to-all-start.2 = ((f32[128,1,128]{2,1,0:T(1,128)}), f32[128,1,128]{2,1,0:T(1,128)S(1)}, u32[]{:S(2)}, u32[]{:S(2)}) async-start(f32[128,1,128]{2,1,0:T(1,128)} %edge.1), calls=%async_computation.2 | async-start | bytes 131072 | tf_op jit(solution)/shard_map/all_to_all | solution.py:558
  113.7 2.9 %collective-permute-done.2.a1_hbm = f32[5,2,128,128]{3,2,1,0:T(8,128)} collective-permute-done((f32[5,2,128,128]{3,2,1,0:T(8,128)S(1)}, f32[5,2,128,128]{3,2,1,0:T(8,128)}, u32[]{:S(2)}, u32[]{:S(2)}) %collective-permute-start.2) | collective-permute-done | bytes 655392 | tf_op jit(solution)/shard_map/ppermute | solution.py:555
  116.6 6.3 %all-to-all-done.2.sums = f32[128,1,128]{2,1,0:T(1,128)S(1)} async-done(((f32[128,1,128]{2,1,0:T(1,128)}), f32[128,1,128]{2,1,0:T(1,128)S(1)}, u32[]{:S(2)}, u32[]{:S(2)}) %all-to-all-start.2) | async-done | bytes 65568 | tf_op jit(solution)/shard_map/all_to_all | solution.py:558
  122.9 0.0 collective-permute-done.1.below_hbm
  122.9 0.0 copy-done.3
  122.9 3.6 %final.1 = f32[4,5,2,128,128]{4,3,2,1,0:T(8,128)} custom-call(s32[4]{0:T(128)S(1)} %copy-done.3, f32[4]{0:T(128)S(1)} %copy-done.4, s32[1]{0:T(128)} %bitcast.where, f32[128,1,128]{2,1,0:T(1,128)S(1)} %all-to-all-done.2.sums, f32[2,5,2,128,128]{4,3,2,1,0:T(8,128)} %collective-permute-done.1.below_hbm, f32[5,2,128,128]{3,2,1,0:T(8,128)S(1)} %inverse.2.refs_5_.s0, ...), custom_call_target="tpu_custom_call" | custom-call | flops 30000000 | bytes 8000000 | tf_op jit(solution)/shard_map/final/pallas_call | solution.py:525
  (2 shorter events, 0.0 us)
Async XLA Ops:
  48.5 36.8 %copy-start = (f32[4,5,2,128,128]{4,3,2,1,0:T(8,128)S(1)}, f32[4,5,2,128,128]{4,3,2,1,0:T(8,128)}, u32[]{:S(2)}) copy-start(f32[4,5,2,128,128]{4,3,2,1,0:T(8,128)} %refs_2_.3) | copy-start | bytes 7864324
  48.5 36.8 %copy-start.1 = (bf16[2,128,384]{2,1,0:T(8,128)(2,1)S(1)}, bf16[2,128,384]{2,1,0:T(8,128)(2,1)}, u32[]{:S(2)}) copy-start(bf16[2,128,384]{2,1,0:T(8,128)(2,1)} %constant.22.clone.refs_4_) | copy-start | bytes 589828
  48.6 36.8 %copy-start.2 = (bf16[256,256]{1,0:T(8,128)(2,1)S(1)}, bf16[256,256]{1,0:T(8,128)(2,1)}, u32[]{:S(2)}) copy-start(bf16[256,256]{1,0:T(8,128)(2,1)} %constant.20.clone.refs_3_) | copy-start | bytes 393220
  86.1 36.8 %copy-start.3 = (s32[4]{0:T(128)S(1)}, s32[4]{0:T(128)}, u32[]{:S(2)}) copy-start(s32[4]{0:T(128)} %centre.1) | copy-start | bytes 52
  86.1 36.8 %copy-start.4 = (f32[4]{0:T(128)S(1)}, f32[4]{0:T(128)}, u32[]{:S(2)}) copy-start(f32[4]{0:T(128)} %positions.1) | copy-start | bytes 52
  88.2 34.7 %collective-permute-start.1 = (f32[2,5,2,128,128]{4,3,2,1,0:T(8,128)S(1)}, f32[2,5,2,128,128]{4,3,2,1,0:T(8,128)}, u32[]{:S(2)}, u32[]{:S(2)}) collective-permute-start(f32[2,5,2,128,128]{4,3,2,1,0:T(8,128)S(1)} %get-tuple-element.15.upper), channel_id=1, source_target_pairs={{0,32},{32,64},{64,96},{1,33},{33,65},{65,97},{2,34},{34,66},{66,9... | collective-permute-start | bytes 3932168 | tf_op jit(solution)/shard_map/ppermute | solution.py:556
  95.9 13.4 %collective-permute-start = (f32[5,2,128,128]{3,2,1,0:T(8,128)S(1)}, f32[5,2,128,128]{3,2,1,0:T(8,128)S(1)}, u32[]{:S(2)}, u32[]{:S(2)}) collective-permute-start(f32[5,2,128,128]{3,2,1,0:T(8,128)S(1)} %inverse.2.refs_5_.s0), channel_id=1, source_target_pairs={{32,0},{64,32},{96,64},{33,1},{65,33},{97,65},{34,2},{66,34},{98,6... | collective-permute-start | bytes 1966088 | tf_op jit(solution)/shard_map/ppermute | solution.py:553
  97.9 18.7 %collective-permute-start.2 = (f32[5,2,128,128]{3,2,1,0:T(8,128)S(1)}, f32[5,2,128,128]{3,2,1,0:T(8,128)}, u32[]{:S(2)}, u32[]{:S(2)}) collective-permute-start(f32[5,2,128,128]{3,2,1,0:T(8,128)S(1)} %get-tuple-element.16.s1), channel_id=1, source_target_pairs={{32,0},{64,32},{96,64},{33,1},{65,33},{97,65},{34,2},{66,34},{98,6... | collective-permute-start | bytes 1966088 | tf_op jit(solution)/shard_map/ppermute | solution.py:555
  110.2 12.7 %all-to-all-start.2 = ((f32[128,1,128]{2,1,0:T(1,128)}), f32[128,1,128]{2,1,0:T(1,128)S(1)}, u32[]{:S(2)}, u32[]{:S(2)}) async-start(f32[128,1,128]{2,1,0:T(1,128)} %edge.1), calls=%async_computation.2 | async-start | bytes 131072 | tf_op jit(solution)/shard_map/all_to_all | solution.py:558
where the time goes:
time: 127 us; the launch traced here: 126 us
  blocking collectives  78.7 us (62%)
  waiting for transfers between devices  18.7 us (15%)
  starting transfers between devices  15.1 us (12%)
  Pallas kernels  13.8 us (11%)
    all_to_all x1, blocking collectives, local(): f = lax.all_to_all(f, 'gz', 0, 0, tiled=True)  41.9 us
    all_to_all x1, blocking collectives, local(): u = lax.all_to_all(u, 'gz', 0, 0, tiled=True)  36.8 us
    ppermute x1, waiting for transfers between devices, local(): a0 = lax.ppermute(s0, 'img', rows_back)  9.55 us
    ppermute x1, starting transfers between devices, local(): below = lax.ppermute(upper, 'img', rows)  7.77 us
    all_to_all x1, waiting for transfers between devices, local(): sums = lax.all_to_all(part, ('img', 'gz'), 0, 0, tiled=True)  6.26 us
    pallas_call x1, Pallas kernels, forward(): pl.pallas_call(forward_kernel, out_shape=(pltpu.VMEM((GROUPS, 2, 2, 5, 8,...  5.52 us
    pallas_call x1, Pallas kernels, final(): pl.pallas_call(final_kernel, out_shape=jax.ShapeDtypeStruct((4, 5, 2, 128...  3.61 us
    all_to_all x1, starting transfers between devices, local(): sums = lax.all_to_all(part, ('img', 'gz'), 0, 0, tiled=True)  3.52 us
  transfers between devices with their start and end apart: 4, of which 3 were waited for; matrix products, arithmetic and copies ran while one was open for 0% of the time, Pallas kernels for 1%

commit v1 on v0

--- a/solution.py
+++ b/solution.py
@@ -243,50 +243,35 @@
 def solve_kernel(f, rho_ref, out, right, work):
     rho = rho_ref[...]
     sigma = rho * rho
-    power = sigma
-    for _ in range(5):
-        power = power * power
-    closing = 1.0 / (1.0 - power)
     shape = (2, 5, 8, 128)
-    zero = jnp.zeros(shape, F32)
     sb = jnp.broadcast_to(sigma, shape)
-    cb = jnp.broadcast_to(closing, shape)
-
-    def ends(s, carry):
-        v, u, p = carry
-        r = f[s, 0] + f[lax.rem(s + 1, GROUPS), 1]
+    powers = [sigma]
+    for _ in range(GROUPS - 1):
+        powers.append(powers[-1] * sigma)
+    closing = jnp.broadcast_to(1.0 / (1.0 - powers[-1]), shape)
+    v = u = None
+    for s in range(GROUPS):
+        r = f[s, 0] + f[(s + 1) % GROUPS, 1]
         right[s] = r
-        return r + sb * v, u + p[None, None] * r, p * sigma
-
-    v, u, _ = lax.fori_loop(0, GROUPS, ends, (zero, zero, jnp.ones((8, 128), F32)))
-    u_last = u * cb
-
-    def up(s, v):
-        v = right[s] + sb * v
+        v = r if s == 0 else r + sb * v
+        u = r if s == 0 else u + powers[s - 1] * r
         work[s] = v
-        return v
-
-    lax.fori_loop(0, GROUPS, up, v * cb)
+    v_last = v * closing
+    u = u * closing
     gain = jnp.broadcast_to(sigma / (1.0 - sigma * sigma), shape)
     back = jnp.broadcast_to((1.0 / SMOOTH) / (rho + 1.0 / rho), shape)
-
-    def put(s, slot, value):
-        out[s, :, :, slot] = value
-
-    def down(n, carry):
-        u, after = carry
-        s = GROUPS - 1 - n
+    after = last = None
+    for s in reversed(range(GROUPS)):
         value = sb * u
-        p = gain * (work[s] + value)
-        put(s, 0, p)
-        put(s + 1, 1, back * (p + after))
-        return right[s] + value, p
-
-    value = sb * u_last
-    last = gain * (work[GROUPS - 1] + value)
-    put(GROUPS - 1, 0, last)
-    _, head = lax.fori_loop(1, GROUPS, down, (right[GROUPS - 1] + value, last))
-    put(0, 1, back * (head + last))
+        p = gain * ((work[s] + powers[s] * v_last) + value)
+        out[s, :, :, 0] = p
+        if after is None:
+            last = p
+        else:
+            out[s + 1, :, :, 1] = back * (p + after)
+        u = right[s] + value
+        after = p
+    out[0, :, :, 1] = back * (after + last)
 
 
 def fold(value):

time: 127 us -> 126 us (level)
  no operation moved by 1% of the time
where the time goes in v1:
time: 126 us
  blocking collectives  78.7 us (62%)
  waiting for transfers between devices  18.7 us (15%)
  starting transfers between devices  15.1 us (12%)
  Pallas kernels  13.4 us (11%)
    all_to_all x1, blocking collectives, local(): f = lax.all_to_all(f, 'gz', 0, 0, tiled=True)  41.9 us
    all_to_all x1, blocking collectives, local(): u = lax.all_to_all(u, 'gz', 0, 0, tiled=True)  36.8 us
    ppermute x1, waiting for transfers between devices, local(): a0 = lax.ppermute(s0, 'img', rows_back)  9.55 us
    ppermute x1, starting transfers between devices, local(): below = lax.ppermute(upper, 'img', rows)  7.76 us
    all_to_all x1, waiting for transfers between devices, local(): sums = lax.all_to_all(part, ('img', 'gz'), 0, 0, tiled=True)  6.26 us
    pallas_call x1, Pallas kernels, forward(): pl.pallas_call(forward_kernel, out_shape=(pltpu.VMEM((GROUPS, 2, 2, 5, 8,...  5.52 us
    pallas_call x1, Pallas kernels, final(): pl.pallas_call(final_kernel, out_shape=jax.ShapeDtypeStruct((4, 5, 2, 128...  3.61 us
    all_to_all x1, starting transfers between devices, local(): sums = lax.all_to_all(part, ('img', 'gz'), 0, 0, tiled=True)  3.52 us
  transfers between devices with their start and end apart: 4, of which 3 were waited for; matrix products, arithmetic and copies ran while one was open for 0% of the time, Pallas kernels for 1%

profile of v1, /device:TPU:1, one launch (start us, length us, event | category | flops | bytes accessed | tf_op | source)
XLA Modules:
  0.0 126.0 jit_solution(12009370994311619915)
XLA Ops:
  0.0 5.5 %forward.1 = (f32[32,2,2,5,8,128]{5,4,3,2,1,0:T(8,128)S(1)}, f32[2,5,32,8,128]{4,3,2,1,0:T(8,128)S(1)}, f32[8,128]{1,0:T(8,128)S(1)}) custom-call(s32[1]{0:T(128)} %bitcast.1.where, f32[4,5,2,128,128]{4,3,2,1,0:T(8,128)} %refs_2_.3, bf16[256,256]{1,0:T(8,128)(2,1)} %constant.19.clone.ty_hbm, bf16[2,128,384]{2,1,0:T(8,128)(2,1)} %constant.21.clone.tx_hbm, ...), custom_call_target="tpu_custom_call" | custom-call | flops 3000000000 | bytes 9000000 | tf_op jit(solution)/shard_map/forward/pallas_call | solution.py:435
  5.5 41.9 %all_to_all.15.f = f32[32,2,2,5,8,128]{5,4,3,2,1,0:T(8,128)S(1)} all-to-all(f32[32,2,2,5,8,128]{5,4,3,2,1,0:T(8,128)S(1)} %get-tuple-element.11), channel_id=1, replica_groups=mesh['img'=4,'gz'=32] {'gz'}, dimensions={0} | all-to-all | bytes 5242880 | tf_op jit(solution)/shard_map/all_to_all | solution.py:534
  47.4 0.7 solve.1
  48.1 0.0 copy-start
  48.1 0.0 copy-start.1
  48.1 0.0 copy-start.2
  48.1 36.8 %all_to_all.16.refs_0_ = f32[32,2,5,2,8,128]{5,4,3,2,1,0:T(8,128)S(1)} all-to-all(f32[32,2,5,2,8,128]{5,4,3,2,1,0:T(8,128)S(1)} %solve.1), channel_id=1, replica_groups=mesh['img'=4,'gz'=32] {'gz'}, dimensions={0} | all-to-all | bytes 5242880 | tf_op jit(solution)/shard_map/all_to_all | solution.py:536
  84.9 0.0 copy-done
  84.9 0.0 copy-done.1
  84.9 0.7 inverse.2.refs_5_.s0
  85.7 0.0 copy-start.3
  85.7 0.0 copy-start.4
  85.7 2.0 %inverse.3 = (f32[5,2,128,128]{3,2,1,0:T(8,128)S(1)}, f32[2,5,2,128,128]{4,3,2,1,0:T(8,128)S(1)}, f32[3,8,128]{2,1,0:T(8,128)S(1)}) custom-call(f32[32,2,5,2,8,128]{5,4,3,2,1,0:T(8,128)S(1)} %all_to_all.16.refs_0_, f32[2,5,32,8,128]{4,3,2,1,0:T(8,128)S(1)} %get-tuple-element.13.refs_1_, f32[4,5,2,128,128]{4,3,2,1,0:T(8,128)S(1)} %copy-done, ...), custom_call_target="tpu_custom_call" | custom-call | flops 3000000000 | bytes 9000000 | tf_op jit(solution)/shard_map/inverse/pallas_call | solution.py:484
  87.7 7.8 %collective-permute-start.1 = (f32[2,5,2,128,128]{4,3,2,1,0:T(8,128)S(1)}, f32[2,5,2,128,128]{4,3,2,1,0:T(8,128)}, u32[]{:S(2)}, u32[]{:S(2)}) collective-permute-start(f32[2,5,2,128,128]{4,3,2,1,0:T(8,128)S(1)} %get-tuple-element.15.upper), channel_id=1, source_target_pairs={{0,32},{32,64},{64,96},{1,33},{33,65},{65,97},{2,34},{34,66},{66,9... | collective-permute-start | bytes 3932168 | tf_op jit(solution)/shard_map/ppermute | solution.py:541
  95.5 1.9 %collective-permute-start = (f32[5,2,128,128]{3,2,1,0:T(8,128)S(1)}, f32[5,2,128,128]{3,2,1,0:T(8,128)S(1)}, u32[]{:S(2)}, u32[]{:S(2)}) collective-permute-start(f32[5,2,128,128]{3,2,1,0:T(8,128)S(1)} %inverse.2.refs_5_.s0), channel_id=1, source_target_pairs={{32,0},{64,32},{96,64},{33,1},{65,33},{97,65},{34,2},{66,34},{98,6... | collective-permute-start | bytes 1966088 | tf_op jit(solution)/shard_map/ppermute | solution.py:538
  97.4 1.9 %collective-permute-start.2 = (f32[5,2,128,128]{3,2,1,0:T(8,128)S(1)}, f32[5,2,128,128]{3,2,1,0:T(8,128)}, u32[]{:S(2)}, u32[]{:S(2)}) collective-permute-start(f32[5,2,128,128]{3,2,1,0:T(8,128)S(1)} %get-tuple-element.16.s1), channel_id=1, source_target_pairs={{32,0},{64,32},{96,64},{33,1},{65,33},{97,65},{34,2},{66,34},{98,6... | collective-permute-start | bytes 1966088 | tf_op jit(solution)/shard_map/ppermute | solution.py:540
  99.4 9.6 %collective-permute-done.above.a0 = f32[5,2,128,128]{3,2,1,0:T(8,128)S(1)} collective-permute-done((f32[5,2,128,128]{3,2,1,0:T(8,128)S(1)}, f32[5,2,128,128]{3,2,1,0:T(8,128)S(1)}, u32[]{:S(2)}, u32[]{:S(2)}) %collective-permute-start) | collective-permute-done | bytes 655392 | tf_op jit(solution)/shard_map/ppermute | solution.py:538
  108.9 0.8 edge.1
  109.8 3.5 %all-to-all-start.2 = ((f32[128,1,128]{2,1,0:T(1,128)}), f32[128,1,128]{2,1,0:T(1,128)S(1)}, u32[]{:S(2)}, u32[]{:S(2)}) async-start(f32[128,1,128]{2,1,0:T(1,128)} %edge.1), calls=%async_computation.2 | async-start | bytes 131072 | tf_op jit(solution)/shard_map/all_to_all | solution.py:543
  113.3 2.9 %collective-permute-done.2.a1_hbm = f32[5,2,128,128]{3,2,1,0:T(8,128)} collective-permute-done((f32[5,2,128,128]{3,2,1,0:T(8,128)S(1)}, f32[5,2,128,128]{3,2,1,0:T(8,128)}, u32[]{:S(2)}, u32[]{:S(2)}) %collective-permute-start.2) | collective-permute-done | bytes 655392 | tf_op jit(solution)/shard_map/ppermute | solution.py:540
  116.2 6.3 %all-to-all-done.2.sums = f32[128,1,128]{2,1,0:T(1,128)S(1)} async-done(((f32[128,1,128]{2,1,0:T(1,128)}), f32[128,1,128]{2,1,0:T(1,128)S(1)}, u32[]{:S(2)}, u32[]{:S(2)}) %all-to-all-start.2) | async-done | bytes 65568 | tf_op jit(solution)/shard_map/all_to_all | solution.py:543
  122.4 0.0 collective-permute-done.1.below_hbm
  122.4 0.0 copy-done.4
  122.4 3.6 %final.1 = f32[4,5,2,128,128]{4,3,2,1,0:T(8,128)} custom-call(s32[4]{0:T(128)S(1)} %copy-done.3, f32[4]{0:T(128)S(1)} %copy-done.4, s32[1]{0:T(128)} %bitcast.where, f32[128,1,128]{2,1,0:T(1,128)S(1)} %all-to-all-done.2.sums, f32[2,5,2,128,128]{4,3,2,1,0:T(8,128)} %collective-permute-done.1.below_hbm, f32[5,2,128,128]{3,2,1,0:T(8,128)S(1)} %inverse.2.refs_5_.s0, ...), custom_call_target="tpu_custom_call" | custom-call | flops 30000000 | bytes 8000000 | tf_op jit(solution)/shard_map/final/pallas_call | solution.py:510
  (2 shorter events, 0.0 us)
Async XLA Ops:
  48.1 36.8 %copy-start = (f32[4,5,2,128,128]{4,3,2,1,0:T(8,128)S(1)}, f32[4,5,2,128,128]{4,3,2,1,0:T(8,128)}, u32[]{:S(2)}) copy-start(f32[4,5,2,128,128]{4,3,2,1,0:T(8,128)} %refs_2_.3) | copy-start | bytes 7864324
  48.1 36.8 %copy-start.1 = (bf16[2,128,384]{2,1,0:T(8,128)(2,1)S(1)}, bf16[2,128,384]{2,1,0:T(8,128)(2,1)}, u32[]{:S(2)}) copy-start(bf16[2,128,384]{2,1,0:T(8,128)(2,1)} %constant.22.clone.refs_4_) | copy-start | bytes 589828
  48.1 36.8 %copy-start.2 = (bf16[256,256]{1,0:T(8,128)(2,1)S(1)}, bf16[256,256]{1,0:T(8,128)(2,1)}, u32[]{:S(2)}) copy-start(bf16[256,256]{1,0:T(8,128)(2,1)} %constant.20.clone.refs_3_) | copy-start | bytes 393220
  85.7 36.8 %copy-start.3 = (s32[4]{0:T(128)S(1)}, s32[4]{0:T(128)}, u32[]{:S(2)}) copy-start(s32[4]{0:T(128)} %centre.1) | copy-start | bytes 52
  85.7 36.8 %copy-start.4 = (f32[4]{0:T(128)S(1)}, f32[4]{0:T(128)}, u32[]{:S(2)}) copy-start(f32[4]{0:T(128)} %positions.1) | copy-start | bytes 52
  87.7 34.7 %collective-permute-start.1 = (f32[2,5,2,128,128]{4,3,2,1,0:T(8,128)S(1)}, f32[2,5,2,128,128]{4,3,2,1,0:T(8,128)}, u32[]{:S(2)}, u32[]{:S(2)}) collective-permute-start(f32[2,5,2,128,128]{4,3,2,1,0:T(8,128)S(1)} %get-tuple-element.15.upper), channel_id=1, source_target_pairs={{0,32},{32,64},{64,96},{1,33},{33,65},{65,97},{2,34},{34,66},{66,9... | collective-permute-start | bytes 3932168 | tf_op jit(solution)/shard_map/ppermute | solution.py:541
  95.5 13.4 %collective-permute-start = (f32[5,2,128,128]{3,2,1,0:T(8,128)S(1)}, f32[5,2,128,128]{3,2,1,0:T(8,128)S(1)}, u32[]{:S(2)}, u32[]{:S(2)}) collective-permute-start(f32[5,2,128,128]{3,2,1,0:T(8,128)S(1)} %inverse.2.refs_5_.s0), channel_id=1, source_target_pairs={{32,0},{64,32},{96,64},{33,1},{65,33},{97,65},{34,2},{66,34},{98,6... | collective-permute-start | bytes 1966088 | tf_op jit(solution)/shard_map/ppermute | solution.py:538
  97.4 18.7 %collective-permute-start.2 = (f32[5,2,128,128]{3,2,1,0:T(8,128)S(1)}, f32[5,2,128,128]{3,2,1,0:T(8,128)}, u32[]{:S(2)}, u32[]{:S(2)}) collective-permute-start(f32[5,2,128,128]{3,2,1,0:T(8,128)S(1)} %get-tuple-element.16.s1), channel_id=1, source_target_pairs={{32,0},{64,32},{96,64},{33,1},{65,33},{97,65},{34,2},{66,34},{98,6... | collective-permute-start | bytes 1966088 | tf_op jit(solution)/shard_map/ppermute | solution.py:540
  109.8 12.7 %all-to-all-start.2 = ((f32[128,1,128]{2,1,0:T(1,128)}), f32[128,1,128]{2,1,0:T(1,128)S(1)}, u32[]{:S(2)}, u32[]{:S(2)}) async-start(f32[128,1,128]{2,1,0:T(1,128)} %edge.1), calls=%async_computation.2 | async-start | bytes 131072 | tf_op jit(solution)/shard_map/all_to_all | solution.py:543

commit v2 on v1

--- a/solution.py
+++ b/solution.py
@@ -358,8 +358,8 @@
     def fetch_a1(c):
         return pltpu.make_async_copy(a1_hbm.at[c], a1.at[c], a1_sem.at[c])
 
-    def store(c):
-        return pltpu.make_async_copy(out.at[c], out_hbm.at[:, c], out_sem.at[c])
+    def store(c, zz):
+        return pltpu.make_async_copy(out.at[c, zz], out_hbm.at[:, c, zz], out_sem.at[c, zz])
 
     for c in range(5):
         fetch_below(c).start()
@@ -401,6 +401,7 @@
     for c in range(5):
         fetch_below(c).wait()
         fetch_a1(c).wait()
+    for c in range(5):
         lines = [below.at[c, 0], below.at[c, 1], s0.at[c], s1.at[c]]
         lines += [upper.at[0, c], upper.at[1, c], a0.at[c], a1.at[c]]
         for zz in range(2):
@@ -411,10 +412,11 @@
                     acc = pieces[m] * weights[m, 0]
                     for r in range(1, 5):
                         acc = acc + pieces[m + r] * weights[m, r]
-                    out[c, m, zz, rows] = acc
-        store(c).start()
+                    out[c, zz, m, rows] = acc
+            store(c, zz).start()
     for c in range(5):
-        store(c).wait()
+        for zz in range(2):
+            store(c, zz).wait()
 
 
 SMEM = pl.BlockSpec(memory_space=pltpu.SMEM)
@@ -515,10 +517,10 @@
         scratch_shapes=[
             pltpu.VMEM((5, 2, 2, 128, 128), F32),
             pltpu.VMEM((5, 2, 128, 128), F32),
-            pltpu.VMEM((5, 4, 2, 128, 128), F32),
+            pltpu.VMEM((5, 2, 4, 128, 128), F32),
             pltpu.SemaphoreType.DMA((5,)),
             pltpu.SemaphoreType.DMA((5,)),
-            pltpu.SemaphoreType.DMA((5,)),
+            pltpu.SemaphoreType.DMA((5, 2)),
         ],
         compiler_params=plain(FINAL_MIB),
         cost_estimate=cost(30_000_000, 8_000_000),

time: 126 us -> 127 us (level)
  no operation moved by 1% of the time
where the time goes in v2:
time: 127 us; the launch traced here: 126 us
  blocking collectives  78.7 us (62%)
  waiting for transfers between devices  18.7 us (15%)
  starting transfers between devices  15.1 us (12%)
  Pallas kernels  13.9 us (11%)
    all_to_all x1, blocking collectives, local(): f = lax.all_to_all(f, 'gz', 0, 0, tiled=True)  41.9 us
    all_to_all x1, blocking collectives, local(): u = lax.all_to_all(u, 'gz', 0, 0, tiled=True)  36.8 us
    ppermute x1, waiting for transfers between devices, local(): a0 = lax.ppermute(s0, 'img', rows_back)  9.55 us
    ppermute x1, starting transfers between devices, local(): below = lax.ppermute(upper, 'img', rows)  7.76 us
    all_to_all x1, waiting for transfers between devices, local(): sums = lax.all_to_all(part, ('img', 'gz'), 0, 0, tiled=True)  6.26 us
    pallas_call x1, Pallas kernels, forward(): pl.pallas_call(forward_kernel, out_shape=(pltpu.VMEM((GROUPS, 2, 2, 5, 8,...  5.52 us
    pallas_call x1, Pallas kernels, final(): pl.pallas_call(final_kernel, out_shape=jax.ShapeDtypeStruct((4, 5, 2, 128...  4.07 us
    all_to_all x1, starting transfers between devices, local(): sums = lax.all_to_all(part, ('img', 'gz'), 0, 0, tiled=True)  3.52 us
  transfers between devices with their start and end apart: 4, of which 3 were waited for; matrix products, arithmetic and copies ran while one was open for 0% of the time, Pallas kernels for 1%

profile of v2, /device:TPU:1, one launch (start us, length us, event | category | flops | bytes accessed | tf_op | source)
XLA Modules:
  0.0 126.5 jit_solution(15881274887726828076)
XLA Ops:
  0.0 5.5 %forward.1 = (f32[32,2,2,5,8,128]{5,4,3,2,1,0:T(8,128)S(1)}, f32[2,5,32,8,128]{4,3,2,1,0:T(8,128)S(1)}, f32[8,128]{1,0:T(8,128)S(1)}) custom-call(s32[1]{0:T(128)} %bitcast.1.where, f32[4,5,2,128,128]{4,3,2,1,0:T(8,128)} %refs_2_.3, bf16[256,256]{1,0:T(8,128)(2,1)} %constant.19.clone.ty_hbm, bf16[2,128,384]{2,1,0:T(8,128)(2,1)} %constant.21.clone.tx_hbm, ...), custom_call_target="tpu_custom_call" | custom-call | flops 3000000000 | bytes 9000000 | tf_op jit(solution)/shard_map/forward/pallas_call | solution.py:437
  5.5 41.9 %all_to_all.15.f = f32[32,2,2,5,8,128]{5,4,3,2,1,0:T(8,128)S(1)} all-to-all(f32[32,2,2,5,8,128]{5,4,3,2,1,0:T(8,128)S(1)} %get-tuple-element.11), channel_id=1, replica_groups=mesh['img'=4,'gz'=32] {'gz'}, dimensions={0} | all-to-all | bytes 5242880 | tf_op jit(solution)/shard_map/all_to_all | solution.py:536
  47.4 0.7 solve.1
  48.1 0.0 copy-start
  48.1 0.0 copy-start.1
  48.1 0.0 copy-start.2
  48.1 36.8 %all_to_all.16.refs_0_ = f32[32,2,5,2,8,128]{5,4,3,2,1,0:T(8,128)S(1)} all-to-all(f32[32,2,5,2,8,128]{5,4,3,2,1,0:T(8,128)S(1)} %solve.1), channel_id=1, replica_groups=mesh['img'=4,'gz'=32] {'gz'}, dimensions={0} | all-to-all | bytes 5242880 | tf_op jit(solution)/shard_map/all_to_all | solution.py:538
  84.9 0.0 copy-done
  84.9 0.0 copy-done.1
  84.9 0.7 inverse.2.refs_5_.s0
  85.7 0.0 copy-start.3
  85.7 0.0 copy-start.4
  85.7 2.0 %inverse.3 = (f32[5,2,128,128]{3,2,1,0:T(8,128)S(1)}, f32[2,5,2,128,128]{4,3,2,1,0:T(8,128)S(1)}, f32[3,8,128]{2,1,0:T(8,128)S(1)}) custom-call(f32[32,2,5,2,8,128]{5,4,3,2,1,0:T(8,128)S(1)} %all_to_all.16.refs_0_, f32[2,5,32,8,128]{4,3,2,1,0:T(8,128)S(1)} %get-tuple-element.13.refs_1_, f32[4,5,2,128,128]{4,3,2,1,0:T(8,128)S(1)} %copy-done, ...), custom_call_target="tpu_custom_call" | custom-call | flops 3000000000 | bytes 9000000 | tf_op jit(solution)/shard_map/inverse/pallas_call | solution.py:486
  87.7 7.8 %collective-permute-start.1 = (f32[2,5,2,128,128]{4,3,2,1,0:T(8,128)S(1)}, f32[2,5,2,128,128]{4,3,2,1,0:T(8,128)}, u32[]{:S(2)}, u32[]{:S(2)}) collective-permute-start(f32[2,5,2,128,128]{4,3,2,1,0:T(8,128)S(1)} %get-tuple-element.15.upper), channel_id=1, source_target_pairs={{0,32},{32,64},{64,96},{1,33},{33,65},{65,97},{2,34},{34,66},{66,9... | collective-permute-start | bytes 3932168 | tf_op jit(solution)/shard_map/ppermute | solution.py:543
  95.5 1.9 %collective-permute-start = (f32[5,2,128,128]{3,2,1,0:T(8,128)S(1)}, f32[5,2,128,128]{3,2,1,0:T(8,128)S(1)}, u32[]{:S(2)}, u32[]{:S(2)}) collective-permute-start(f32[5,2,128,128]{3,2,1,0:T(8,128)S(1)} %inverse.2.refs_5_.s0), channel_id=1, source_target_pairs={{32,0},{64,32},{96,64},{33,1},{65,33},{97,65},{34,2},{66,34},{98,6... | collective-permute-start | bytes 1966088 | tf_op jit(solution)/shard_map/ppermute | solution.py:540
  97.4 1.9 %collective-permute-start.2 = (f32[5,2,128,128]{3,2,1,0:T(8,128)S(1)}, f32[5,2,128,128]{3,2,1,0:T(8,128)}, u32[]{:S(2)}, u32[]{:S(2)}) collective-permute-start(f32[5,2,128,128]{3,2,1,0:T(8,128)S(1)} %get-tuple-element.16.s1), channel_id=1, source_target_pairs={{32,0},{64,32},{96,64},{33,1},{65,33},{97,65},{34,2},{66,34},{98,6... | collective-permute-start | bytes 1966088 | tf_op jit(solution)/shard_map/ppermute | solution.py:542
  99.4 9.6 %collective-permute-done.above.a0 = f32[5,2,128,128]{3,2,1,0:T(8,128)S(1)} collective-permute-done((f32[5,2,128,128]{3,2,1,0:T(8,128)S(1)}, f32[5,2,128,128]{3,2,1,0:T(8,128)S(1)}, u32[]{:S(2)}, u32[]{:S(2)}) %collective-permute-start) | collective-permute-done | bytes 655392 | tf_op jit(solution)/shard_map/ppermute | solution.py:540
  108.9 0.8 edge.1
  109.8 3.5 %all-to-all-start.2 = ((f32[128,1,128]{2,1,0:T(1,128)}), f32[128,1,128]{2,1,0:T(1,128)S(1)}, u32[]{:S(2)}, u32[]{:S(2)}) async-start(f32[128,1,128]{2,1,0:T(1,128)} %edge.1), calls=%async_computation.2 | async-start | bytes 131072 | tf_op jit(solution)/shard_map/all_to_all | solution.py:545
  113.3 2.9 %collective-permute-done.2.a1_hbm = f32[5,2,128,128]{3,2,1,0:T(8,128)} collective-permute-done((f32[5,2,128,128]{3,2,1,0:T(8,128)S(1)}, f32[5,2,128,128]{3,2,1,0:T(8,128)}, u32[]{:S(2)}, u32[]{:S(2)}) %collective-permute-start.2) | collective-permute-done | bytes 655392 | tf_op jit(solution)/shard_map/ppermute | solution.py:542
  116.2 6.3 %all-to-all-done.2.sums = f32[128,1,128]{2,1,0:T(1,128)S(1)} async-done(((f32[128,1,128]{2,1,0:T(1,128)}), f32[128,1,128]{2,1,0:T(1,128)S(1)}, u32[]{:S(2)}, u32[]{:S(2)}) %all-to-all-start.2) | async-done | bytes 65568 | tf_op jit(solution)/shard_map/all_to_all | solution.py:545
  122.4 0.0 collective-permute-done.1.below_hbm
  122.4 0.0 copy-done.4
  122.4 4.1 %final.1 = f32[4,5,2,128,128]{4,3,2,1,0:T(8,128)} custom-call(s32[4]{0:T(128)S(1)} %copy-done.3, f32[4]{0:T(128)S(1)} %copy-done.4, s32[1]{0:T(128)} %bitcast.where, f32[128,1,128]{2,1,0:T(1,128)S(1)} %all-to-all-done.2.sums, f32[2,5,2,128,128]{4,3,2,1,0:T(8,128)} %collective-permute-done.1.below_hbm, f32[5,2,128,128]{3,2,1,0:T(8,128)S(1)} %inverse.2.refs_5_.s0, ...), custom_call_target="tpu_custom_call" | custom-call | flops 30000000 | bytes 8000000 | tf_op jit(solution)/shard_map/final/pallas_call | solution.py:512
  (2 shorter events, 0.0 us)
Async XLA Ops:
  48.1 36.8 %copy-start = (f32[4,5,2,128,128]{4,3,2,1,0:T(8,128)S(1)}, f32[4,5,2,128,128]{4,3,2,1,0:T(8,128)}, u32[]{:S(2)}) copy-start(f32[4,5,2,128,128]{4,3,2,1,0:T(8,128)} %refs_2_.3) | copy-start | bytes 7864324
  48.1 36.8 %copy-start.1 = (bf16[2,128,384]{2,1,0:T(8,128)(2,1)S(1)}, bf16[2,128,384]{2,1,0:T(8,128)(2,1)}, u32[]{:S(2)}) copy-start(bf16[2,128,384]{2,1,0:T(8,128)(2,1)} %constant.22.clone.refs_4_) | copy-start | bytes 589828
  48.1 36.8 %copy-start.2 = (bf16[256,256]{1,0:T(8,128)(2,1)S(1)}, bf16[256,256]{1,0:T(8,128)(2,1)}, u32[]{:S(2)}) copy-start(bf16[256,256]{1,0:T(8,128)(2,1)} %constant.20.clone.refs_3_) | copy-start | bytes 393220
  85.7 36.8 %copy-start.3 = (s32[4]{0:T(128)S(1)}, s32[4]{0:T(128)}, u32[]{:S(2)}) copy-start(s32[4]{0:T(128)} %centre.1) | copy-start | bytes 52
  85.7 36.8 %copy-start.4 = (f32[4]{0:T(128)S(1)}, f32[4]{0:T(128)}, u32[]{:S(2)}) copy-start(f32[4]{0:T(128)} %positions.1) | copy-start | bytes 52
  87.7 34.7 %collective-permute-start.1 = (f32[2,5,2,128,128]{4,3,2,1,0:T(8,128)S(1)}, f32[2,5,2,128,128]{4,3,2,1,0:T(8,128)}, u32[]{:S(2)}, u32[]{:S(2)}) collective-permute-start(f32[2,5,2,128,128]{4,3,2,1,0:T(8,128)S(1)} %get-tuple-element.15.upper), channel_id=1, source_target_pairs={{0,32},{32,64},{64,96},{1,33},{33,65},{65,97},{2,34},{34,66},{66,9... | collective-permute-start | bytes 3932168 | tf_op jit(solution)/shard_map/ppermute | solution.py:543
  95.5 13.4 %collective-permute-start = (f32[5,2,128,128]{3,2,1,0:T(8,128)S(1)}, f32[5,2,128,128]{3,2,1,0:T(8,128)S(1)}, u32[]{:S(2)}, u32[]{:S(2)}) collective-permute-start(f32[5,2,128,128]{3,2,1,0:T(8,128)S(1)} %inverse.2.refs_5_.s0), channel_id=1, source_target_pairs={{32,0},{64,32},{96,64},{33,1},{65,33},{97,65},{34,2},{66,34},{98,6... | collective-permute-start | bytes 1966088 | tf_op jit(solution)/shard_map/ppermute | solution.py:540
  97.4 18.7 %collective-permute-start.2 = (f32[5,2,128,128]{3,2,1,0:T(8,128)S(1)}, f32[5,2,128,128]{3,2,1,0:T(8,128)}, u32[]{:S(2)}, u32[]{:S(2)}) collective-permute-start(f32[5,2,128,128]{3,2,1,0:T(8,128)S(1)} %get-tuple-element.16.s1), channel_id=1, source_target_pairs={{32,0},{64,32},{96,64},{33,1},{65,33},{97,65},{34,2},{66,34},{98,6... | collective-permute-start | bytes 1966088 | tf_op jit(solution)/shard_map/ppermute | solution.py:542
  109.8 12.7 %all-to-all-start.2 = ((f32[128,1,128]{2,1,0:T(1,128)}), f32[128,1,128]{2,1,0:T(1,128)S(1)}, u32[]{:S(2)}, u32[]{:S(2)}) async-start(f32[128,1,128]{2,1,0:T(1,128)} %edge.1), calls=%async_computation.2 | async-start | bytes 131072 | tf_op jit(solution)/shard_map/all_to_all | solution.py:545
